TPU v7x, 32 devices: a whole 2x2x4 slice. The times are simulated.
32 devices in a mesh: groups: 2 (over y), feat: 4 (over z), dp: 2 (over x), section: 2 (over core).
Axes of the slice: x: 2, y: 2, z: 4, core: 2. Of those that a mesh axis runs over, the one named last changes fastest.
Arguments:
- residuals: bfloat16 [2, 3072, 8192], P('section', ('groups', 'dp'), 'feat'), parts along dimension 1, may hold values from -6 to 6
- final_resid: bfloat16 [3072, 8192], P(('groups', 'dp', 'section'), 'feat'), parts along dimension 0, may hold values from -6 to 6
- final_order: int32 [3072], P(('groups', 'dp')), parts along dimension 0, may hold values from 0 to 767, as said below
- translator: bfloat16 [2, 8192, 8192], P('section', 'dp', 'feat'), may hold values from -0.0625 to 0.0625
- bias: float32 [2, 8192], P('section', 'feat'), may hold values from -5 to 5
Outputs:
- grad_weight: bfloat16 [4, 8192, 8192], P(('groups', 'section'), 'dp', 'feat'), parts along dimension 0
- grad_bias: float32 [4, 8192], P(('groups', 'section'), 'feat'), parts along dimension 0
There are 2 independent parts, one for each index of `groups`. A program takes and returns all parts, laid end to end along the dimension named above; an argument that names none is the same for every part. Nothing has to cross between parts.
Inputs may be any that keep to these rules, and one draw needn't show every extreme that they name: Within each aligned block of 768 tokens final_order is a permutation of 0 to 767.
All inputs are finite; a program needn't handle non-finite values.
Results may differ from a plain program's by a relative error of at most 0.0058.
Values may be sent and summed in bfloat16 or wider, within the bound.
A program may use at most 192 MiB of HBM per device.

v0:
```python
import math
import jax
import jax.numpy as jnp
from jax import lax
from jax.sharding import PartitionSpec as P

CHUNKS = 2


def on_device(residuals, final_resid, final_order, translator, bias):
    own = residuals[0]
    weight = translator[0]
    tokens = own.shape[0]
    ways = lax.axis_size("dp")
    factor = 1.0 / math.sqrt(tokens * ways)
    gathered_final = lax.all_gather(final_resid, "section", axis=0, tiled=True)
    targets = gathered_final[final_order].astype(jnp.float32)
    step = tokens // CHUNKS
    inputs, errors = ([], [])
    grad_b = 0.0
    for c in range(CHUNKS):
        rows = slice(c * step, (c + 1) * step)
        wide = lax.all_gather(own[rows], "feat", axis=1, tiled=True)
        halves = jnp.stack(jnp.split(wide, ways, axis=1))
        mine = lax.all_to_all(halves, "dp", split_axis=0, concat_axis=0, tiled=True)
        mine = mine.reshape(ways * step, -1)
        part = jnp.dot(mine, weight, preferred_element_type=jnp.float32).astype(jnp.bfloat16)
        parts = lax.all_to_all(
            part.reshape(ways, step, -1), "dp", split_axis=0, concat_axis=0, tiled=True
        )
        product = jnp.sum(parts.astype(jnp.float32), axis=0)
        scaled = (own[rows].astype(jnp.float32) + product + bias[0] - targets[rows]) * factor
        grad_b = grad_b + jnp.sum(scaled, axis=0)
        inputs.append(mine)
        errors.append(lax.all_gather(scaled.astype(jnp.bfloat16), "dp", axis=0, tiled=True))
    grad_b = lax.psum(grad_b, "dp")
    grad_w = lax.dot_general(
        jnp.concatenate(inputs),
        jnp.concatenate(errors),
        (((0,), (0,)), ((), ())),
        preferred_element_type=jnp.float32,
    ).astype(jnp.bfloat16)
    return (grad_w[None], grad_b[None])


def solution(mesh):
    placed = (
        P("section", ("groups", "dp"), "feat"),
        P(("groups", "dp", "section"), "feat"),
        P(("groups", "dp")),
        P("section", "dp", "feat"),
        P("section", "feat"),
    )
    return jax.shard_map(
        on_device,
        mesh=mesh,
        in_specs=placed,
        out_specs=(P(("groups", "section"), "dp", "feat"), P(("groups", "section"), "feat")),
        check_vma=False,
    )
```

profile of v0, /device:TPU:0, one launch (start us, length us, event | category | flops | bytes accessed | tf_op | source)
XLA Modules:
  0.0 546.1 jit_solution(4865078908594601578)
XLA Ops:
  7.2 4.0 fusion.25
  12.0 117.5 %all-gather.14.cloned.1.call-done = bf16[1,384,8192]{2,1,0:T(8,128)(2,1)} async-done(((bf16[1,384,2048]{2,1,0:T(8,128)(2,1)}), bf16[1,384,8192]{2,1,0:T(8,128)(2,1)}) %all-gather.14.cloned.1.call-update) | async-done | bytes 6291472 | tf_op jit(solution)/shard_map/all_gather | solution.py:23
  129.4 3.3 slice_bitcast_fusion.3
  132.7 3.1 pad_maximum_fusion
  135.8 6.5 %all-to-all-start = ((bf16[2,384,4096]{2,1,0:T(8,128)(2,1)}), bf16[2,384,4096]{2,1,0:T(8,128)(2,1)}, u32[]{:S(2)}, u32[]{:S(2)}) async-start(bf16[2,384,4096]{2,1,0:T(8,128)(2,1)} %pad_maximum_fusion), calls=%async_computation | async-start | bytes 12582912 | tf_op jit(solution)/shard_map/all_to_all | solution.py:25
  143.0 101.5 %all-gather.16.cloned.1.call-done = bf16[1,384,8192]{2,1,0:T(8,128)(2,1)} async-done(((bf16[1,384,2048]{2,1,0:T(8,128)(2,1)}), bf16[1,384,8192]{2,1,0:T(8,128)(2,1)}) %all-gather.16.cloned.1.call-update) | async-done | bytes 6291472 | tf_op jit(solution)/shard_map/all_gather | solution.py:23
  244.6 3.3 slice_bitcast_fusion.1
  247.8 3.2 pad_maximum_fusion.1
  251.1 6.8 %all-to-all-start.1 = ((bf16[2,384,4096]{2,1,0:T(8,128)(2,1)}), bf16[2,384,4096]{2,1,0:T(8,128)(2,1)}, u32[]{:S(2)}, u32[]{:S(2)}) async-start(bf16[2,384,4096]{2,1,0:T(8,128)(2,1)} %pad_maximum_fusion.1), calls=%async_computation.1 | async-start | bytes 12582912 | tf_op jit(solution)/shard_map/all_to_all | solution.py:25
  257.9 19.7 %fusion.10 = bf16[768,2048]{1,0:T(8,128)(2,1)} fusion(bf16[768,4096]{1,0:T(8,128)(2,1)} %bitcast.3, bf16[1,4096,2048]{2,1,0:T(8,128)(2,1)} %param.8), kind=kOutput, calls=%fused_computation.16 | convolution fusion | flops 12886474752 | bytes 26214400 | tf_op jit(solution)/shard_map/dot_general | solution.py:27
  277.6 50.7 %all-to-all-done.1 = bf16[2,384,4096]{2,1,0:T(8,128)(2,1)} async-done(((bf16[2,384,4096]{2,1,0:T(8,128)(2,1)}), bf16[2,384,4096]{2,1,0:T(8,128)(2,1)}, u32[]{:S(2)}, u32[]{:S(2)}) %all-to-all-start.1) | async-done | bytes 6291488 | tf_op jit(solution)/shard_map/all_to_all | solution.py:25
  328.3 4.1 all-to-all-start.2
  332.4 19.7 %fusion.13 = bf16[768,2048]{1,0:T(8,128)(2,1)} fusion(bf16[768,4096]{1,0:T(8,128)(2,1)} %bitcast.7, bf16[1,4096,2048]{2,1,0:T(8,128)(2,1)} %param.8), kind=kOutput, calls=%fused_computation.17 | convolution fusion | flops 12886474752 | bytes 26214400 | tf_op jit(solution)/shard_map/dot_general | solution.py:27
  352.2 15.9 %all-to-all-done.2 = bf16[2,384,2048]{2,1,0:T(8,128)(2,1)S(1)} async-done(((bf16[2,384,2048]{2,1,0:T(8,128)(2,1)}), bf16[2,384,2048]{2,1,0:T(8,128)(2,1)S(1)}, u32[]{:S(2)}, u32[]{:S(2)}) %all-to-all-start.2) | async-done | bytes 3145760 | tf_op jit(solution)/shard_map/all_to_all | solution.py:28
  369.7 5.2 all-to-all-start.3
  375.0 8.6 %gather_fusion = bf16[768,2048]{1,0:T(8,128)(2,1)S(1)} fusion(bf16[768,2048]{1,0:T(8,128)(2,1)} %all-gather.8.cloned.1.call-done, s32[1024]{0:T(1024)S(1)} %pad_clamp_fusion), kind=kCustom, calls=%fused_computation | custom fusion | bytes 6294528 | tf_op jit(solution)/shard_map/gather | solution.py:17
  383.7 3.5 convert_element_type.33
  389.6 20.2 %all-to-all-done.3 = bf16[2,384,2048]{2,1,0:T(8,128)(2,1)} async-done(((bf16[2,384,2048]{2,1,0:T(8,128)(2,1)}), bf16[2,384,2048]{2,1,0:T(8,128)(2,1)}, u32[]{:S(2)}, u32[]{:S(2)}) %all-to-all-start.3) | async-done | bytes 3145760 | tf_op jit(solution)/shard_map/all_to_all | solution.py:28
  409.9 3.2 convert_reduce_fusion
  413.6 4.7 fusion.23
  418.9 5.8 %psum.7 = f32[1,2048]{1,0:T(1,128)} all-reduce(f32[1,2048]{1,0:T(1,128)S(1)} %bitcast.47), channel_id=1, replica_groups=mesh['groups'=2,'feat'=4,'dp'=2,'section'=2] {'dp'}, use_global_device_ids=true, to_apply=%region_4.0 | all-reduce | flops 2048 | bytes 16384 | tf_op jit(solution)/shard_map/psum | solution.py:36
  424.7 35.5 %all-gather.12.cloned.1.call-done = bf16[768,2048]{1,0:T(8,128)(2,1)} async-done(((bf16[384,2048]{1,0:T(8,128)(2,1)}), bf16[768,2048]{1,0:T(8,128)(2,1)}) %all-gather.12.cloned.1.call-update) | async-done | bytes 3145744 | tf_op jit(solution)/shard_map/all_gather | solution.py:35
  460.2 46.4 %all-gather.10.cloned.1.call-done = bf16[768,2048]{1,0:T(8,128)(2,1)} async-done(((bf16[384,2048]{1,0:T(8,128)(2,1)}), bf16[768,2048]{1,0:T(8,128)(2,1)}) %all-gather.10.cloned.1.call-update) | async-done | bytes 3145744 | tf_op jit(solution)/shard_map/all_gather | solution.py:35
  506.5 33.0 %convert_bitcast_fusion = bf16[1,4096,2048]{2,1,0:T(8,128)(2,1)} fusion(bf16[768,4096]{1,0:T(8,128)(2,1)} %bitcast.7, bf16[768,4096]{1,0:T(8,128)(2,1)} %bitcast.3, bf16[768,2048]{1,0:T(8,128)(2,1)} %all-gather.12.cloned.1.call-done, bf16[768,2048]{1,0:T(8,128)(2,1)} %all-gather.10.cloned.1.call-done), kind=kOutput, calls=%fused_computation.5 | convolution fusion | flops 25815941120 | bytes 35651584 | tf_op jit(solution)/shard_map/dot_general | solution.py:37
  (28 shorter events, 6.8 us)
Async XLA Ops:
  7.2 122.3 %all-gather.14.cloned.1.call-start = ((), (), s32[]{:S(2)}) async-start(), calls=%async_computation.7 | async-start | bytes 7864320 | tf_op jit(solution)/shard_map/all_gather | solution.py:23
  11.2 233.3 %all-gather.16.cloned.1.call-start = ((), (), s32[]{:S(2)}) async-start(), calls=%async_computation.8 | async-start | bytes 7864320 | tf_op jit(solution)/shard_map/all_gather | solution.py:23
  135.8 115.3 %all-to-all-start = ((bf16[2,384,4096]{2,1,0:T(8,128)(2,1)}), bf16[2,384,4096]{2,1,0:T(8,128)(2,1)}, u32[]{:S(2)}, u32[]{:S(2)}) async-start(bf16[2,384,4096]{2,1,0:T(8,128)(2,1)} %pad_maximum_fusion), calls=%async_computation | async-start | bytes 12582912 | tf_op jit(solution)/shard_map/all_to_all | solution.py:25
  142.3 232.7 %all-gather.8.cloned.1.call-start = ((), (), s32[]{:S(2)}) async-start(), calls=%async_computation.4 | async-start | bytes 4718592 | tf_op jit(solution)/shard_map/all_gather | solution.py:16
  251.1 77.2 %all-to-all-start.1 = ((bf16[2,384,4096]{2,1,0:T(8,128)(2,1)}), bf16[2,384,4096]{2,1,0:T(8,128)(2,1)}, u32[]{:S(2)}, u32[]{:S(2)}) async-start(bf16[2,384,4096]{2,1,0:T(8,128)(2,1)} %pad_maximum_fusion.1), calls=%async_computation.1 | async-start | bytes 12582912 | tf_op jit(solution)/shard_map/all_to_all | solution.py:25
  328.3 39.7 %all-to-all-start.2 = ((bf16[2,384,2048]{2,1,0:T(8,128)(2,1)}), bf16[2,384,2048]{2,1,0:T(8,128)(2,1)S(1)}, u32[]{:S(2)}, u32[]{:S(2)}) async-start(bf16[2,384,2048]{2,1,0:T(8,128)(2,1)} %bitcast.46), calls=%async_computation.2 | async-start | bytes 6291456 | tf_op jit(solution)/shard_map/all_to_all | solution.py:28
  368.0 1.7 copy-start.2
  368.0 6.9 %copy-start.5 = (s32[768]{0:T(1024)S(1)}, s32[768]{0:T(1024)}, u32[]{:S(2)}) copy-start(s32[768]{0:T(1024)} %param.7) | copy-start | bytes 9220
  369.7 40.1 %all-to-all-start.3 = ((bf16[2,384,2048]{2,1,0:T(8,128)(2,1)}), bf16[2,384,2048]{2,1,0:T(8,128)(2,1)}, u32[]{:S(2)}, u32[]{:S(2)}) async-start(bf16[2,384,2048]{2,1,0:T(8,128)(2,1)} %bitcast.45), calls=%async_computation.3 | async-start | bytes 6291456 | tf_op jit(solution)/shard_map/all_to_all | solution.py:28
  374.9 85.3 %all-gather.12.cloned.1.call-start = ((), (), s32[]{:S(2)}) async-start(), calls=%async_computation.6 | async-start | bytes 4718592 | tf_op jit(solution)/shard_map/all_gather | solution.py:35
  383.7 3.6 copy-start.3
  387.2 25.8 %copy-start.1 = (bf16[1,768,2048]{2,1,0:T(8,128)(2,1)S(1)}, bf16[1,768,2048]{2,1,0:T(8,128)(2,1)}, u32[]{:S(2)}) copy-start(bf16[1,768,2048]{2,1,0:T(8,128)(2,1)} %param.5) | copy-start | bytes 9437188
  387.2 25.8 %copy-start.4 = (f32[1,2048]{1,0:T(1,128)S(1)}, f32[1,2048]{1,0:T(1,128)}, u32[]{:S(2)}) copy-start(f32[1,2048]{1,0:T(1,128)} %param.9) | copy-start | bytes 24580
  409.9 3.7 copy-start
  418.3 88.3 %all-gather.10.cloned.1.call-start = ((), (), s32[]{:S(2)}) async-start(), calls=%async_computation.5 | async-start | bytes 4718592 | tf_op jit(solution)/shard_map/all_gather | solution.py:35
Sparse Core Ops, SparseCore 0:
  11.3 118.0 all-gather.13
  131.0 113.5 all-gather.15
  246.1 10.3 all-gather.7
  418.4 41.7 all-gather.11
  461.6 44.9 all-gather.9
where the time goes:
time: 547 us; the launch traced here: 546 us
  waiting for transfers between devices  390 us (71%)
  matrix products  72.4 us (13%)
  starting transfers between devices  22.8 us (4%)
  local copies, waits for them, and re-layouts  21.4 us (4%)
  other arithmetic  20.2 us (4%)
  between operations  13.9 us (3%)
  blocking collectives  5.82 us (1%)
    all_gather x2, waiting for transfers between devices, on_device(): wide = lax.all_gather(own[rows], 'feat', axis=1, tiled=True)  219 us
    all_gather x2, waiting for transfers between devices, on_device(): lax.all_gather(scaled.astype(jnp.bfloat16), 'dp', axis=0, tiled=True)  81.8 us
    all_to_all x2, waiting for transfers between devices, on_device(): mine = lax.all_to_all(halves, 'dp', split_axis=0, concat_axis=0, tiled=True)  50.7 us
    dot_general x2, matrix products, on_device(): jnp.dot(mine, weight, preferred_element_type=jnp.float32)  39.4 us
    all_to_all x2, waiting for transfers between devices, on_device(): lax.all_to_all(part.reshape(ways, step, -1), 'dp', split_axis=0, concat_a...  36.1 us
    dot_general x1, matrix products, on_device(): lax.dot_general(jnp.concatenate(inputs), jnp.concatenate(errors), (((0,),...  33 us
    all_to_all x2, starting transfers between devices, on_device(): mine = lax.all_to_all(halves, 'dp', split_axis=0, concat_axis=0, tiled=True)  13.3 us
  transfers between devices with their start and end apart: 9, of which 7 were waited for; matrix products, arithmetic and copies ran while one was open for 12% of the time, Pallas kernels for 0%

commit v1 on v0

--- a/solution.py
+++ b/solution.py
@@ -20,7 +20,26 @@
     grad_b = 0.0
     for c in range(CHUNKS):
         rows = slice(c * step, (c + 1) * step)
-        wide = lax.all_gather(own[rows], "feat", axis=1, tiled=True)
+        size, position, rows_2 = (lax.axis_size("feat"), lax.axis_index("feat"), own[rows].shape[1])
+        right = [(i, (i + 1) % size) for i in range(size)]
+        left = [(i, (i - 1) % size) for i in range(size)]
+        filled = jnp.zeros(
+            (*own[rows].shape[:1], size * rows_2, *own[rows].shape[1 + 1 :]), own[rows].dtype
+        )
+        filled = lax.dynamic_update_slice_in_dim(filled, own[rows], position * rows_2, axis=1)
+        from_left = from_right = own[rows]
+        halfway = size // 2
+        for turn in range(1, halfway + 1):
+            from_left = lax.ppermute(from_left, "feat", right)
+            filled = lax.dynamic_update_slice_in_dim(
+                filled, from_left, (position - turn) % size * rows_2, axis=1
+            )
+            if turn < size - halfway:
+                from_right = lax.ppermute(from_right, "feat", left)
+                filled = lax.dynamic_update_slice_in_dim(
+                    filled, from_right, (position + turn) % size * rows_2, axis=1
+                )
+        wide = filled
         halves = jnp.stack(jnp.split(wide, ways, axis=1))
         mine = lax.all_to_all(halves, "dp", split_axis=0, concat_axis=0, tiled=True)
         mine = mine.reshape(ways * step, -1)

time: 547 us -> 594 us (1.086)
  starting transfers between devices: 22.8 us -> 96.6 us
  waiting for transfers between devices: 390 us -> 337 us
  local copies, waits for them, and re-layouts: 21.4 us -> 42.9 us
    all_gather x2 -> x0, waiting for transfers between devices: 219 us -> none  [on_device(): wide = lax.all_gather(own[rows], 'feat', axis=1, tiled=True)]
    ppermute x0 -> x6, waiting for transfers between devices: none -> 115 us  [the longest x4 115 us: on_device(): from_left = lax.ppermute(from_left, 'feat', right)]
    ppermute x0 -> x6, starting transfers between devices: none -> 73.2 us  [the longest x4 70.7 us: on_device(): from_left = lax.ppermute(from_left, 'feat', right)]
    all_to_all x2, waiting for transfers between devices: 50.7 us -> 111 us  [on_device(): mine = lax.all_to_all(halves, 'dp', split_axis=0, concat_axis=0, tiled=True)]
    dynamic_update_slice x0 -> x7, local copies, waits for them, and re-layouts: none -> 15.6 us  [the longest x3 7.48 us: on_device(): lax.dynamic_update_slice_in_dim(filled, from_left, (position - turn) % si...]
    all_to_all x2, waiting for transfers between devices: 36.1 us -> 27.7 us  [on_device(): lax.all_to_all(part.reshape(ways, step, -1), 'dp', split_axis=0, concat_a...]
    another operation x0 -> x2, local copies, waits for them, and re-layouts: none -> 6.82 us
  transfers between devices with their start and end apart: 9 -> 13, of which waited for: 7 -> 10; matrix products, arithmetic and copies ran while one was open for 12% -> 14% of each run, Pallas kernels for 0% -> 0%
where the time goes in v1:
time: 594 us; the launch traced here: 593 us
  waiting for transfers between devices  337 us (57%)
  starting transfers between devices  96.6 us (16%)
  matrix products  72.3 us (12%)
  local copies, waits for them, and re-layouts  42.9 us (7%)
  other arithmetic  24.3 us (4%)
  between operations  13.9 us (2%)
    ppermute x4, waiting for transfers between devices, on_device(): from_left = lax.ppermute(from_left, 'feat', right)  115 us
    all_to_all x2, waiting for transfers between devices, on_device(): mine = lax.all_to_all(halves, 'dp', split_axis=0, concat_axis=0, tiled=True)  111 us
    all_gather x2, waiting for transfers between devices, on_device(): lax.all_gather(scaled.astype(jnp.bfloat16), 'dp', axis=0, tiled=True)  82.1 us
    ppermute x4, starting transfers between devices, on_device(): from_left = lax.ppermute(from_left, 'feat', right)  70.7 us
    dot_general x2, matrix products, on_device(): jnp.dot(mine, weight, preferred_element_type=jnp.float32)  39.3 us
    dot_general x1, matrix products, on_device(): lax.dot_general(jnp.concatenate(inputs), jnp.concatenate(errors), (((0,),...  33 us
    all_to_all x2, waiting for transfers between devices, on_device(): lax.all_to_all(part.reshape(ways, step, -1), 'dp', split_axis=0, concat_a...  27.7 us
    all_to_all x2, starting transfers between devices, on_device(): mine = lax.all_to_all(halves, 'dp', split_axis=0, concat_axis=0, tiled=True)  12.6 us
  transfers between devices with their start and end apart: 13, of which 10 were waited for; matrix products, arithmetic and copies ran while one was open for 14% of the time, Pallas kernels for 0%

profile of v1, /device:TPU:0, one launch (start us, length us, event | category | flops | bytes accessed | tf_op | source)
XLA Modules:
  0.0 593.1 jit_solution(4075748290795590033)
XLA Ops:
  7.2 4.0 slice_bitcast_fusion.5
  23.0 28.9 %collective-permute-done = bf16[384,2048]{1,0:T(8,128)(2,1)} collective-permute-done((bf16[384,2048]{1,0:T(8,128)(2,1)}, bf16[384,2048]{1,0:T(8,128)(2,1)}, u32[]{:S(2)}, u32[]{:S(2)}) %collective-permute-start) | collective-permute-done | bytes 1572896 | tf_op jit(solution)/shard_map/ppermute | solution.py:33
  51.9 33.6 %collective-permute-done.3 = bf16[384,2048]{1,0:T(8,128)(2,1)} collective-permute-done((bf16[384,2048]{1,0:T(8,128)(2,1)}, bf16[384,2048]{1,0:T(8,128)(2,1)}, u32[]{:S(2)}, u32[]{:S(2)}) %collective-permute-start.3) | collective-permute-done | bytes 1572896 | tf_op jit(solution)/shard_map/ppermute | solution.py:33
  85.5 66.1 %collective-permute-start.5 = (bf16[384,2048]{1,0:T(8,128)(2,1)}, bf16[384,2048]{1,0:T(8,128)(2,1)S(1)}, u32[]{:S(2)}, u32[]{:S(2)}) collective-permute-start(bf16[384,2048]{1,0:T(8,128)(2,1)} %collective-permute-done.3), channel_id=1, source_target_pairs={{0,4},{4,8},{8,12},{12,0},{1,5},{5,9},{9,13},{13,1},{2,6},{6,10},{... | collective-permute-start | bytes 4718600 | tf_op jit(solution)/shard_map/ppermute | solution.py:33
  167.2 19.3 %collective-permute-done.2 = bf16[384,2048]{1,0:T(8,128)(2,1)S(1)} collective-permute-done((bf16[384,2048]{1,0:T(8,128)(2,1)}, bf16[384,2048]{1,0:T(8,128)(2,1)S(1)}, u32[]{:S(2)}, u32[]{:S(2)}) %collective-permute-start.2) | collective-permute-done | bytes 1572896 | tf_op jit(solution)/shard_map/ppermute | solution.py:33
  186.5 32.9 %collective-permute-done.5 = bf16[384,2048]{1,0:T(8,128)(2,1)S(1)} collective-permute-done((bf16[384,2048]{1,0:T(8,128)(2,1)}, bf16[384,2048]{1,0:T(8,128)(2,1)S(1)}, u32[]{:S(2)}, u32[]{:S(2)}) %collective-permute-start.5) | collective-permute-done | bytes 1572896 | tf_op jit(solution)/shard_map/ppermute | solution.py:33
  227.8 6.3 %all-to-all-start.1 = ((bf16[2,384,4096]{2,1,0:T(8,128)(2,1)}), bf16[2,384,4096]{2,1,0:T(8,128)(2,1)}, u32[]{:S(2)}, u32[]{:S(2)}) async-start(bf16[2,384,4096]{2,1,0:T(8,128)(2,1)} %pad_maximum_fusion.1), calls=%async_computation.1 | async-start | bytes 12582912 | tf_op jit(solution)/shard_map/all_to_all | solution.py:44
  241.3 62.4 %all-to-all-done.1 = bf16[2,384,4096]{2,1,0:T(8,128)(2,1)} async-done(((bf16[2,384,4096]{2,1,0:T(8,128)(2,1)}), bf16[2,384,4096]{2,1,0:T(8,128)(2,1)}, u32[]{:S(2)}, u32[]{:S(2)}) %all-to-all-start.1) | async-done | bytes 6291488 | tf_op jit(solution)/shard_map/all_to_all | solution.py:44
  303.7 6.3 %all-to-all-start = ((bf16[2,384,4096]{2,1,0:T(8,128)(2,1)}), bf16[2,384,4096]{2,1,0:T(8,128)(2,1)}, u32[]{:S(2)}, u32[]{:S(2)}) async-start(bf16[2,384,4096]{2,1,0:T(8,128)(2,1)} %pad_maximum_fusion), calls=%async_computation | async-start | bytes 12582912 | tf_op jit(solution)/shard_map/all_to_all | solution.py:44
  310.1 19.6 %fusion.13 = bf16[768,2048]{1,0:T(8,128)(2,1)} fusion(bf16[768,4096]{1,0:T(8,128)(2,1)} %bitcast.7, bf16[1,4096,2048]{2,1,0:T(8,128)(2,1)} %param.8), kind=kOutput, calls=%fused_computation.17 | convolution fusion | flops 12886474752 | bytes 26214400 | tf_op jit(solution)/shard_map/dot_general | solution.py:46
  329.7 49.0 %all-to-all-done = bf16[2,384,4096]{2,1,0:T(8,128)(2,1)} async-done(((bf16[2,384,4096]{2,1,0:T(8,128)(2,1)}), bf16[2,384,4096]{2,1,0:T(8,128)(2,1)}, u32[]{:S(2)}, u32[]{:S(2)}) %all-to-all-start) | async-done | bytes 6291488 | tf_op jit(solution)/shard_map/all_to_all | solution.py:44
  378.7 5.4 all-to-all-start.3
  384.1 19.7 %fusion.10 = bf16[768,2048]{1,0:T(8,128)(2,1)} fusion(bf16[768,4096]{1,0:T(8,128)(2,1)} %bitcast.3, bf16[1,4096,2048]{2,1,0:T(8,128)(2,1)} %param.8), kind=kOutput, calls=%fused_computation.16 | convolution fusion | flops 12886474752 | bytes 26214400 | tf_op jit(solution)/shard_map/dot_general | solution.py:46
  403.8 14.2 %all-to-all-done.3 = bf16[2,384,2048]{2,1,0:T(8,128)(2,1)} async-done(((bf16[2,384,2048]{2,1,0:T(8,128)(2,1)}), bf16[2,384,2048]{2,1,0:T(8,128)(2,1)}, u32[]{:S(2)}, u32[]{:S(2)}) %all-to-all-start.3) | async-done | bytes 3145760 | tf_op jit(solution)/shard_map/all_to_all | solution.py:47
  417.9 5.4 all-to-all-start.2
  423.4 9.4 %gather_fusion = bf16[768,2048]{1,0:T(8,128)(2,1)} fusion(bf16[768,2048]{1,0:T(8,128)(2,1)} %all-gather.4.cloned.1.call-done, s32[1024]{0:T(1024)S(1)} %pad_clamp_fusion), kind=kCustom, calls=%fused_computation | custom fusion | bytes 6294528 | tf_op jit(solution)/shard_map/gather | solution.py:17
  432.8 5.4 convert_element_type.33
  438.3 4.6 convert_reduce_fusion
  442.9 13.6 %all-to-all-done.2 = bf16[2,384,2048]{2,1,0:T(8,128)(2,1)} async-done(((bf16[2,384,2048]{2,1,0:T(8,128)(2,1)}), bf16[2,384,2048]{2,1,0:T(8,128)(2,1)}, u32[]{:S(2)}, u32[]{:S(2)}) %all-to-all-start.2) | async-done | bytes 3145760 | tf_op jit(solution)/shard_map/all_to_all | solution.py:47
  460.2 4.7 fusion.21
  465.6 5.8 psum.7
  471.4 35.6 %all-gather.8.cloned.1.call-done = bf16[768,2048]{1,0:T(8,128)(2,1)} async-done(((bf16[384,2048]{1,0:T(8,128)(2,1)}), bf16[768,2048]{1,0:T(8,128)(2,1)}) %all-gather.8.cloned.1.call-update) | async-done | bytes 3145744 | tf_op jit(solution)/shard_map/all_gather | solution.py:54
  507.0 46.5 %all-gather.6.cloned.1.call-done = bf16[768,2048]{1,0:T(8,128)(2,1)} async-done(((bf16[384,2048]{1,0:T(8,128)(2,1)}), bf16[768,2048]{1,0:T(8,128)(2,1)}) %all-gather.6.cloned.1.call-update) | async-done | bytes 3145744 | tf_op jit(solution)/shard_map/all_gather | solution.py:54
  553.5 33.0 %convert_bitcast_fusion = bf16[1,4096,2048]{2,1,0:T(8,128)(2,1)} fusion(bf16[768,4096]{1,0:T(8,128)(2,1)} %bitcast.7, bf16[768,4096]{1,0:T(8,128)(2,1)} %bitcast.3, bf16[768,2048]{1,0:T(8,128)(2,1)} %all-gather.8.cloned.1.call-done, bf16[768,2048]{1,0:T(8,128)(2,1)} %all-gather.6.cloned.1.call-done), kind=kOutput, calls=%fused_computation.5 | convolution fusion | flops 25815941120 | bytes 35651584 | tf_op jit(solution)/shard_map/dot_general | solution.py:56
  (39 shorter events, 47.7 us)
Async XLA Ops:
  11.1 40.7 %collective-permute-start = (bf16[384,2048]{1,0:T(8,128)(2,1)}, bf16[384,2048]{1,0:T(8,128)(2,1)}, u32[]{:S(2)}, u32[]{:S(2)}) collective-permute-start(bf16[384,2048]{1,0:T(8,128)(2,1)} %get-tuple-element.10), channel_id=1, source_target_pairs={{0,4},{4,8},{8,12},{12,0},{1,5},{5,9},{9,13},{13,1},{2,6},{6,10},{... | collective-permute-start | bytes 4718600 | tf_op jit(solution)/shard_map/ppermute | solution.py:33
  14.2 71.3 %collective-permute-start.3 = (bf16[384,2048]{1,0:T(8,128)(2,1)}, bf16[384,2048]{1,0:T(8,128)(2,1)}, u32[]{:S(2)}, u32[]{:S(2)}) collective-permute-start(bf16[384,2048]{1,0:T(8,128)(2,1)} %get-tuple-element.11), channel_id=1, source_target_pairs={{0,4},{4,8},{8,12},{12,0},{1,5},{5,9},{9,13},{13,1},{2,6},{6,10},{... | collective-permute-start | bytes 4718600 | tf_op jit(solution)/shard_map/ppermute | solution.py:33
  15.7 148.8 %collective-permute-start.1 = (bf16[384,2048]{1,0:T(8,128)(2,1)}, bf16[384,2048]{1,0:T(8,128)(2,1)}, u32[]{:S(2)}, u32[]{:S(2)}) collective-permute-start(bf16[384,2048]{1,0:T(8,128)(2,1)} %get-tuple-element.10), channel_id=1, source_target_pairs={{0,12},{4,0},{8,4},{12,8},{1,13},{5,1},{9,5},{13,9},{2,14},{6,2},{... | collective-permute-start | bytes 4718600 | tf_op jit(solution)/shard_map/ppermute | solution.py:38
  18.0 143.8 %collective-permute-start.4 = (bf16[384,2048]{1,0:T(8,128)(2,1)}, bf16[384,2048]{1,0:T(8,128)(2,1)}, u32[]{:S(2)}, u32[]{:S(2)}) collective-permute-start(bf16[384,2048]{1,0:T(8,128)(2,1)} %get-tuple-element.11), channel_id=1, source_target_pairs={{0,12},{4,0},{8,4},{12,8},{1,13},{5,1},{9,5},{13,9},{2,14},{6,2},{... | collective-permute-start | bytes 4718600 | tf_op jit(solution)/shard_map/ppermute | solution.py:38
  18.3 3.5 copy-start
  51.9 134.6 %collective-permute-start.2 = (bf16[384,2048]{1,0:T(8,128)(2,1)}, bf16[384,2048]{1,0:T(8,128)(2,1)S(1)}, u32[]{:S(2)}, u32[]{:S(2)}) collective-permute-start(bf16[384,2048]{1,0:T(8,128)(2,1)} %collective-permute-done), channel_id=1, source_target_pairs={{0,4},{4,8},{8,12},{12,0},{1,5},{5,9},{9,13},{13,1},{2,6},{6,10},{... | collective-permute-start | bytes 4718600 | tf_op jit(solution)/shard_map/ppermute | solution.py:33
  85.5 133.9 %collective-permute-start.5 = (bf16[384,2048]{1,0:T(8,128)(2,1)}, bf16[384,2048]{1,0:T(8,128)(2,1)S(1)}, u32[]{:S(2)}, u32[]{:S(2)}) collective-permute-start(bf16[384,2048]{1,0:T(8,128)(2,1)} %collective-permute-done.3), channel_id=1, source_target_pairs={{0,4},{4,8},{8,12},{12,0},{1,5},{5,9},{9,13},{13,1},{2,6},{6,10},{... | collective-permute-start | bytes 4718600 | tf_op jit(solution)/shard_map/ppermute | solution.py:33
  227.8 75.9 %all-to-all-start.1 = ((bf16[2,384,4096]{2,1,0:T(8,128)(2,1)}), bf16[2,384,4096]{2,1,0:T(8,128)(2,1)}, u32[]{:S(2)}, u32[]{:S(2)}) async-start(bf16[2,384,4096]{2,1,0:T(8,128)(2,1)} %pad_maximum_fusion.1), calls=%async_computation.1 | async-start | bytes 12582912 | tf_op jit(solution)/shard_map/all_to_all | solution.py:44
  234.1 189.3 %all-gather.4.cloned.1.call-start = ((), (), s32[]{:S(2)}) async-start(), calls=%async_computation.4 | async-start | bytes 4718592 | tf_op jit(solution)/shard_map/all_gather | solution.py:16
  303.7 75.0 %all-to-all-start = ((bf16[2,384,4096]{2,1,0:T(8,128)(2,1)}), bf16[2,384,4096]{2,1,0:T(8,128)(2,1)}, u32[]{:S(2)}, u32[]{:S(2)}) async-start(bf16[2,384,4096]{2,1,0:T(8,128)(2,1)} %pad_maximum_fusion), calls=%async_computation | async-start | bytes 12582912 | tf_op jit(solution)/shard_map/all_to_all | solution.py:44
  378.7 39.2 %all-to-all-start.3 = ((bf16[2,384,2048]{2,1,0:T(8,128)(2,1)}), bf16[2,384,2048]{2,1,0:T(8,128)(2,1)}, u32[]{:S(2)}, u32[]{:S(2)}) async-start(bf16[2,384,2048]{2,1,0:T(8,128)(2,1)} %bitcast.44), calls=%async_computation.3 | async-start | bytes 6291456 | tf_op jit(solution)/shard_map/all_to_all | solution.py:47
  417.9 5.4 copy-start.3
  417.9 38.5 %all-to-all-start.2 = ((bf16[2,384,2048]{2,1,0:T(8,128)(2,1)}), bf16[2,384,2048]{2,1,0:T(8,128)(2,1)}, u32[]{:S(2)}, u32[]{:S(2)}) async-start(bf16[2,384,2048]{2,1,0:T(8,128)(2,1)} %bitcast.43), calls=%async_computation.2 | async-start | bytes 6291456 | tf_op jit(solution)/shard_map/all_to_all | solution.py:47
  423.3 83.7 %all-gather.8.cloned.1.call-start = ((), (), s32[]{:S(2)}) async-start(), calls=%async_computation.6 | async-start | bytes 4718592 | tf_op jit(solution)/shard_map/all_gather | solution.py:54
  438.3 21.4 %copy-start.2 = (f32[1,2048]{1,0:T(1,128)S(1)}, f32[1,2048]{1,0:T(1,128)}, u32[]{:S(2)}) copy-start(f32[1,2048]{1,0:T(1,128)} %param.9) | copy-start | bytes 24580
  456.4 3.7 copy-start.1
  464.8 88.7 %all-gather.6.cloned.1.call-start = ((), (), s32[]{:S(2)}) async-start(), calls=%async_computation.5 | async-start | bytes 4718592 | tf_op jit(solution)/shard_map/all_gather | solution.py:54
Sparse Core Ops, SparseCore 0:
  236.5 11.8 all-gather.3
  465.0 41.9 all-gather.7
  508.5 44.9 all-gather.5
